TPU v7x, 32 devices: a whole 2x2x4 slice. The times are simulated.
32 devices in a mesh: groups: 2 (over y), space: 4 (over z), tm: 2 (over x), freq: 2 (over core).
Axes of the slice: x: 2, y: 2, z: 4, core: 2. Of those that a mesh axis runs over, the one named last changes fastest.
Arguments:
- snapshots: float32 [16, 64, 16384], P(None, 'space', ('groups', 'tm')), parts along dimension 2, may hold values from -28 to 28, as said below
- weights: float32 [16384], P(('groups', 'tm', 'space')), parts along dimension 0, may hold values from 0.3 to 3
Outputs:
- modes: float32 [16, 2, 16, 16384], P('freq', None, None, ('groups', 'tm', 'space')), parts along dimension 3
- r_factor: float32 [4, 16, 16, 16], P('groups', 'freq'), parts along dimension 0
There are 2 independent parts, one for each index of `groups`. A program takes and returns all parts, laid end to end along the dimension named above; each array names one. Nothing has to cross between parts.
Inputs may be any that keep to these rules, and one draw needn't show every extreme that they name: `snapshots`: velocity fluctuations of the jet.
All inputs are finite; a program needn't handle non-finite values.
Results may differ from a plain program's by a relative error of at most 0.00009.
Values sent between devices are 32-bit elements; how exact they have to be, the bound alone decides.
A program may use at most 64 MiB of HBM per device.

v0:
```python
import functools

import jax
import jax.numpy as jnp
import numpy as np
from jax import lax
from jax.experimental import pallas as pl
from jax.experimental.pallas import tpu as pltpu
from jax.sharding import PartitionSpec as P

SEGMENT_FRAMES = 64
NF = 16
GROUP = 4

epsilon = 1e-05
MESH = pl.DeviceIdType.MESH
HIGHEST = lax.Precision.HIGHEST


def dft_table(half, senders, local_times):
    moments = np.arange(SEGMENT_FRAMES)
    hann = 0.5 - 0.5 * np.cos(2.0 * np.pi * moments / SEGMENT_FRAMES)
    taper = hann / np.sqrt(np.sum(hann * hann))
    angle = (np.arange(NF) + 1)[:, None] * moments[None, :] % SEGMENT_FRAMES
    phase = 2.0 * np.pi * angle / SEGMENT_FRAMES
    pair = np.stack([np.cos(phase) * taper, -np.sin(phase) * taper])
    pair = pair.reshape(2, NF // half, half, senders, local_times)
    full = np.einsum("rhfzt,bc->hrbfzct", pair, np.eye(GROUP))
    shape = (NF // half, 2 * GROUP * half, senders * GROUP * local_times)
    return full.reshape(shape).astype(np.float32)


def xor(a, d, bits):
    out = a
    for k in range(bits):
        if d >> k & 1:
            bit = lax.rem(lax.div(a, 1 << k), 2)
            out = out + (1 << k) - (2 << k) * bit
    return out


def peers_along(me, count):
    bits = count.bit_length() - 1
    if count == 1 << bits:
        order = sorted(range(1, count), key=lambda d: -(d.bit_length()))
        return [xor(me, d, bits) for d in order]
    return [lax.rem(me + d, count) for d in range(1, count)]


def spectra_kernel(
    exchange, space, tm, total, snap, weight, table, x_out, g_out,
    recv, spec, away, g_send, g_recv,
    s_send, s_recv, l_sem, p_send, p_recv, gs_sem, gr_sem,
):
    core = lax.axis_index("freq")
    z = lax.axis_index("space")
    other = 1 - core
    rows = recv.shape[3]
    chunks = recv.shape[1] // GROUP
    half = spec.shape[3]
    z_peers = peers_along(z, space)
    m = lax.axis_index("tm")
    m_peers = peers_along(m, tm)
    g_peers = [(m, p) for p in z_peers] + [(o, p) for o in m_peers for p in [*z_peers, z]]

    def cols(p):
        return pl.ds(pl.multiple_of((p * 2 + core) * rows, rows), rows)

    def blocks(q):
        return pl.ds(q * GROUP, GROUP)

    def local(q):
        if exchange:
            source, slot = snap.at[blocks(q), :, cols(z)], z
        else:
            source, slot = snap.at[blocks(q)], 0
        return pltpu.make_async_copy(source, recv.at[slot, blocks(q)], l_sem.at[q])

    def send(q, i):
        return pltpu.make_async_remote_copy(
            src_ref=snap.at[blocks(q), :, cols(z_peers[i])],
            dst_ref=recv.at[z, blocks(q)],
            send_sem=s_send.at[q, i],
            recv_sem=s_recv.at[q, z],
            device_id={"space": z_peers[i]},
            device_id_type=MESH,
        )

    def arrive(q, i):
        p = z_peers[i]
        return pltpu.make_async_remote_copy(
            src_ref=snap.at[blocks(q), :, cols(p)],
            dst_ref=recv.at[p, blocks(q)],
            send_sem=s_send.at[q, i],
            recv_sem=s_recv.at[q, p],
            device_id={"space": p},
            device_id_type=MESH,
        )

    def trade(q, row):
        return pltpu.make_async_remote_copy(
            src_ref=away.at[q],
            dst_ref=spec.at[row, :, blocks(q)],
            send_sem=p_send.at[q],
            recv_sem=p_recv.at[q],
            device_id={"freq": other},
            device_id_type=MESH,
        )

    def gram_copy(i, slot):
        o, p = g_peers[i]
        return pltpu.make_async_remote_copy(
            src_ref=g_send,
            dst_ref=g_recv.at[slot],
            send_sem=gs_sem.at[i],
            recv_sem=gr_sem.at[slot],
            device_id={"space": p, "tm": o},
            device_id_type=MESH,
        )

    barrier = pltpu.get_barrier_semaphore()
    pl.semaphore_signal(barrier, inc=1, device_id={"freq": other}, device_id_type=MESH)
    for o, p in g_peers:
        pl.semaphore_signal(
            barrier, inc=1, device_id={"space": p, "tm": o}, device_id_type=MESH
        )
    for q in range(chunks):
        local(q).start()
    pl.semaphore_wait(barrier, 1 + len(g_peers))

    hops = range(len(z_peers)) if exchange else range(0)
    for q in range(chunks):
        for i in hops:
            send(q, i).start()

    both = jnp.concatenate([table[core], table[other]], axis=0)
    for q in range(chunks):
        local(q).wait()
        for i in hops:
            arrive(q, i).wait_recv()
        flat = recv[:, q * GROUP : (q + 1) * GROUP].reshape(-1, rows)
        got = jnp.dot(both, flat, precision=HIGHEST, preferred_element_type=jnp.float32)
        got = got.reshape(2, 2, GROUP, half, rows)
        away[q] = got[1]
        trade(q, core).start()
        spec[core, :, q * GROUP : (q + 1) * GROUP] = got[0]

    def gram(c):
        one = spec[c].reshape(-1, rows)
        return lax.dot_general(
            one * weight[c], one, (((1,), (1,)), ((), ())),
            precision=HIGHEST, preferred_element_type=jnp.float32,
        )

    product = gram(core)
    for q in range(chunks):
        trade(q, other).wait_recv()
    product = product + gram(other)
    n = product.shape[0] // 2
    pair = (
        product[:n, :n] + product[n:, n:],
        product[:n, n:] - product[n:, :n],
    )
    shape = (n // half, half, n)
    same = lax.rem(lax.broadcasted_iota(jnp.int32, shape, 2), half) == (
        lax.broadcasted_iota(jnp.int32, shape, 1)
    )
    for r in range(2):
        g_send[r] = jnp.sum(jnp.where(same, pair[r].reshape(shape), 0.0), axis=1)
    mine = m * space + z
    for i in range(len(g_peers)):
        gram_copy(i, mine).start()
    g_recv[mine] = g_send[...]
    for c in range(2):
        x_out[:, c * rows : (c + 1) * rows] = spec[c].reshape(-1, rows)
    for q in range(chunks):
        trade(q, core).wait_send()
        for i in hops:
            send(q, i).wait_send()
    for i, (o, p) in enumerate(g_peers):
        gram_copy(i, o * space + p).wait_recv()
    for i in range(len(g_peers)):
        gram_copy(i, mine).wait_send()
    acc = g_recv[0]
    for s in range(1, space * tm):
        acc = acc + g_recv[s]
    g_out[...] = acc * (1.0 / total)


def modes_kernel(half, gram, x, modes, upper):
    nb, lanes = gram.shape[1], gram.shape[2]
    row = lax.broadcasted_iota(jnp.int32, (nb, lanes), 0)
    lane = lax.broadcasted_iota(jnp.int32, (nb, lanes), 1)
    col = lane // half
    which = lane % half

    def pick(a, index):
        return jnp.take_along_axis(a, index, axis=1, mode="promise_in_bounds")

    re = gram[0] + jnp.where(row == col, epsilon, 0.0)
    im = gram[1]
    diag = jnp.zeros_like(re)
    for p in range(nb):
        index = which + p * half
        cr, ci = pick(re, index), pick(im, index)
        diag = jnp.where(row == p, cr, diag)
        if p == nb - 1:
            break
        inv = 1.0 / cr[p : p + 1]
        mr, mi = cr * inv, ci * inv
        pr, pi = re[p : p + 1], im[p : p + 1]
        here = col == p
        nr = jnp.where(here, 0.0, re) - (
            mr * jnp.where(here[:1], 1.0, pr) - mi * jnp.where(here[:1], 0.0, pi)
        )
        ni = jnp.where(here, 0.0, im) - (
            mr * jnp.where(here[:1], 0.0, pi) + mi * jnp.where(here[:1], 1.0, pr)
        )
        re = jnp.where(row > p, nr, re)
        im = jnp.where(row > p, ni, im)
    pivot = jnp.sqrt(diag)
    scale = 1.0 / pivot
    re, im = re * scale, im * scale
    ur = jnp.where(col > row, re, jnp.where(col == row, pivot, 0.0))
    ui = jnp.where(col > row, im, 0.0)
    lr = jnp.where(col < row, re, jnp.where(col == row, scale, 0.0))
    li = jnp.where(col < row, im, 0.0)
    for f in range(half):
        index = (lane * half + f) % lanes
        upper[0, f] = pick(ur, index)[:, :nb]
        upper[1, f] = pick(ui, index)[:, :nb]
    parts = []
    for f in range(half):
        fr = jnp.where(which == f, lr, 0.0)
        fi = jnp.where(which == f, li, 0.0)
        parts.append(jnp.concatenate([fr, fi], axis=1))
        parts.append(jnp.concatenate([-fi, fr], axis=1))
    big = jnp.concatenate(parts, axis=0)
    out = jnp.dot(big, x[...], precision=HIGHEST, preferred_element_type=jnp.float32)
    modes[...] = out.reshape(modes.shape)


def on_device(snapshots, weights):
    freq = lax.axis_size("freq")
    space = lax.axis_size("space")
    tm = lax.axis_size("tm")
    assert freq == 2
    half = NF // freq
    nb, local_times, columns = snapshots.shape
    rows = columns // (space * freq)
    exchange = local_times % 8 == 0
    if not exchange:
        shaped = snapshots.reshape(nb, local_times, space, freq, rows)
        own = lax.dynamic_index_in_dim(shaped, lax.axis_index("freq"), 3, keepdims=False)
        pieces = lax.all_to_all(own, "space", split_axis=2, concat_axis=1, tiled=True)
        snapshots = pieces.reshape(nb, SEGMENT_FRAMES, rows)
    senders = space if exchange else 1
    times = SEGMENT_FRAMES // senders
    chunks = nb // GROUP
    table = jnp.asarray(dft_table(half, senders, times))
    weight = weights.reshape(freq, 1, rows)
    lanes = nb * half
    peers = space * tm
    vmem = pl.BlockSpec(memory_space=pltpu.VMEM)
    dma = pltpu.SemaphoreType.DMA
    x, gram = pl.pallas_call(
        functools.partial(
            spectra_kernel, exchange, space, tm, weights.shape[0] * space * tm
        ),
        out_shape=(
            jax.ShapeDtypeStruct((2 * lanes, freq * rows), jnp.float32),
            jax.ShapeDtypeStruct((2, nb, lanes), jnp.float32),
        ),
        in_specs=[pl.BlockSpec(memory_space=pl.ANY), vmem, vmem],
        out_specs=(vmem, vmem),
        scratch_shapes=[
            pltpu.VMEM((senders, nb, times, rows), jnp.float32),
            pltpu.VMEM((freq, 2, nb, half, rows), jnp.float32),
            pltpu.VMEM((chunks, 2, GROUP, half, rows), jnp.float32),
            pltpu.VMEM((2, nb, lanes), jnp.float32),
            pltpu.VMEM((peers, 2, nb, lanes), jnp.float32),
            dma((chunks, max(space - 1, 1))),
            dma((chunks, space)),
            dma((chunks,)),
            dma((chunks,)),
            dma((chunks,)),
            dma((peers,)),
            dma((peers,)),
        ],
        compiler_params=pltpu.CompilerParams(
            collective_id=0, has_side_effects=True, vmem_limit_bytes=40 * 2**20
        ),
        name="spectra",
    )(snapshots, weight, table)
    modes, upper = pl.pallas_call(
        functools.partial(modes_kernel, half),
        out_shape=(
            jax.ShapeDtypeStruct((half, 2, nb, freq * rows), jnp.float32),
            jax.ShapeDtypeStruct((2, half, nb, nb), jnp.float32),
        ),
        in_specs=[vmem, vmem],
        out_specs=(vmem, vmem),
        compiler_params=pltpu.CompilerParams(vmem_limit_bytes=40 * 2**20),
        name="modes",
    )(gram, x)
    return modes, upper


def solution(mesh):
    return jax.shard_map(
        on_device,
        mesh=mesh,
        in_specs=(P(None, "space", ("groups", "tm")), P(("groups", "tm", "space"))),
        out_specs=(
            P("freq", None, None, ("groups", "tm", "space")),
            P("groups", "freq", None, None),
        ),
        check_vma=False,
    )
```

profile of v0, /device:TPU:0, one launch (start us, length us, event | category | flops | bytes accessed | tf_op | source)
XLA Modules:
  0.0 66.3 jit_solution(1856329793561961215)
XLA Ops:
  0.6 0.0 copy-start
  0.6 2.2 %copy-done = f32[16,16,4096]{2,1,0:T(8,128)S(1)} copy-done((f32[16,16,4096]{2,1,0:T(8,128)S(1)}, f32[16,16,4096]{2,1,0:T(8,128)}, u32[]{:S(2)}) %copy-start) | copy-done | bytes 4194328
  2.8 0.0 copy-start.1
  2.8 0.9 %copy-done.1 = f32[2,64,256]{2,1,0:T(8,128)S(1)} copy-done((f32[2,64,256]{2,1,0:T(8,128)S(1)}, f32[2,64,256]{2,1,0:T(8,128)}, u32[]{:S(2)}) %copy-start.1) | copy-done | bytes 131096
  3.7 0.0 copy-start.2
  3.7 0.7 %copy-done.2 = f32[1024]{0:T(1024)S(1)} copy-done((f32[1024]{0:T(1024)S(1)}, f32[1024]{0:T(1024)}, u32[]{:S(2)}) %copy-start.2) | copy-done | bytes 4120
  4.4 58.6 %spectra.1 = (f32[256,1024]{1,0:T(8,128)S(1)}, f32[2,16,128]{2,1,0:T(8,128)S(1)}) custom-call(f32[16,16,4096]{2,1,0:T(8,128)S(1)} %copy-done, f32[2,1,512]{2,1,0:T(1,128)S(1)} %bitcast.1, f32[2,64,256]{2,1,0:T(8,128)S(1)} %copy-done.1), custom_call_target="tpu_custom_call" | custom-call | tf_op jit(solution)/shard_map/spectra/pallas_call | solution.py:266
  63.0 3.3 %modes.1 = (f32[8,2,16,1024]{3,2,1,0:T(8,128)}, f32[2,8,16,16]{3,2,1,0:T(8,128)}) custom-call(f32[2,16,128]{2,1,0:T(8,128)S(1)} %get-tuple-element.4.gram, f32[256,1024]{1,0:T(8,128)S(1)} %get-tuple-element.5.x), custom_call_target="tpu_custom_call" | custom-call | tf_op jit(solution)/shard_map/modes/pallas_call | solution.py:295
Async XLA Ops:
  0.6 2.2 %copy-start = (f32[16,16,4096]{2,1,0:T(8,128)S(1)}, f32[16,16,4096]{2,1,0:T(8,128)}, u32[]{:S(2)}) copy-start(f32[16,16,4096]{2,1,0:T(8,128)} %snap.1) | copy-start | bytes 12582916
  2.8 0.9 %copy-start.1 = (f32[2,64,256]{2,1,0:T(8,128)S(1)}, f32[2,64,256]{2,1,0:T(8,128)}, u32[]{:S(2)}) copy-start(f32[2,64,256]{2,1,0:T(8,128)} %constant.2.clone.table) | copy-start | bytes 393220
  3.7 0.7 %copy-start.2 = (f32[1024]{0:T(1024)S(1)}, f32[1024]{0:T(1024)}, u32[]{:S(2)}) copy-start(f32[1024]{0:T(1024)} %param.4) | copy-start | bytes 12292
where the time goes:
time: 66.5 us; the launch traced here: 66.3 us
  Pallas kernels  61.8 us (93%)
  local copies, waits for them, and re-layouts  3.77 us (6%)
    pallas_call x1, Pallas kernels, on_device(): pl.pallas_call(functools.partial(spectra_kernel, exchange, space, tm, wei...  58.6 us
    unnamed x6, local copies, waits for them, and re-layouts  3.77 us
    pallas_call x1, Pallas kernels, on_device(): pl.pallas_call(functools.partial(modes_kernel, half), out_shape=(jax.Shap...  3.26 us

commit v1 on v0

--- a/solution.py
+++ b/solution.py
@@ -31,26 +31,30 @@
 
 
 def xor(a, d, bits):
-    out = a
+    out = 0
     for k in range(bits):
-        if d >> k & 1:
-            bit = lax.rem(lax.div(a, 1 << k), 2)
-            out = out + (1 << k) - (2 << k) * bit
+        first = lax.rem(lax.div(a, 1 << k), 2)
+        second = lax.rem(lax.div(d, 1 << k), 2)
+        out = out + (1 << k) * (first + second - 2 * first * second)
     return out
 
 
-def peers_along(me, count):
+def peers_along(me, count, late):
     bits = count.bit_length() - 1
-    if count == 1 << bits:
-        order = sorted(range(1, count), key=lambda d: -(d.bit_length()))
-        return [xor(me, d, bits) for d in order]
-    return [lax.rem(me + d, count) for d in range(1, count)]
+    if count != 1 << bits:
+        return [lax.rem(me + d, count) for d in range(1, count)]
+    near = list(range(1, count // 2))
+    far = list(range(count // 2, count))
+    early, after = far + near, near + far
+    return [
+        xor(me, a + late * (b - a), bits) for a, b in zip(early, after)
+    ]
 
 
 def spectra_kernel(
-    exchange, space, tm, total, snap, weight, table, x_out, g_out,
-    recv, spec, away, g_send, g_recv,
-    s_send, s_recv, l_sem, p_send, p_recv, gs_sem, gr_sem,
+    exchange, space, tm, total, snap, weight_in, table_in, x_out, g_out,
+    weight, table, recv, spec, away, g_send, g_recv,
+    c_sem, s_send, s_recv, l_sem, p_send, p_recv, gs_sem, gr_sem,
 ):
     core = lax.axis_index("freq")
     z = lax.axis_index("space")
@@ -58,9 +62,9 @@
     rows = recv.shape[3]
     chunks = recv.shape[1] // GROUP
     half = spec.shape[3]
-    z_peers = peers_along(z, space)
+    z_peers = peers_along(z, space, 0)
     m = lax.axis_index("tm")
-    m_peers = peers_along(m, tm)
+    m_peers = peers_along(m, tm, 0)
     g_peers = [(m, p) for p in z_peers] + [(o, p) for o in m_peers for p in [*z_peers, z]]
 
     def cols(p):
@@ -124,15 +128,23 @@
         pl.semaphore_signal(
             barrier, inc=1, device_id={"space": p, "tm": o}, device_id_type=MESH
         )
-    for q in range(chunks):
-        local(q).start()
+    constants = [
+        pltpu.make_async_copy(weight_in, weight, c_sem.at[0]),
+        pltpu.make_async_copy(table_in, table, c_sem.at[1]),
+    ]
+    for copy in constants:
+        copy.start()
     pl.semaphore_wait(barrier, 1 + len(g_peers))
 
     hops = range(len(z_peers)) if exchange else range(0)
     for q in range(chunks):
         for i in hops:
             send(q, i).start()
-
+    for q in range(chunks):
+        local(q).start()
+
+    for copy in constants:
+        copy.wait()
     both = jnp.concatenate([table[core], table[other]], axis=0)
     for q in range(chunks):
         local(q).wait()
@@ -271,14 +283,17 @@
             jax.ShapeDtypeStruct((2 * lanes, freq * rows), jnp.float32),
             jax.ShapeDtypeStruct((2, nb, lanes), jnp.float32),
         ),
-        in_specs=[pl.BlockSpec(memory_space=pl.ANY), vmem, vmem],
+        in_specs=[pl.BlockSpec(memory_space=pltpu.HBM)] * 3,
         out_specs=(vmem, vmem),
         scratch_shapes=[
+            pltpu.VMEM(weight.shape, jnp.float32),
+            pltpu.VMEM(table.shape, jnp.float32),
             pltpu.VMEM((senders, nb, times, rows), jnp.float32),
             pltpu.VMEM((freq, 2, nb, half, rows), jnp.float32),
             pltpu.VMEM((chunks, 2, GROUP, half, rows), jnp.float32),
             pltpu.VMEM((2, nb, lanes), jnp.float32),
             pltpu.VMEM((peers, 2, nb, lanes), jnp.float32),
+            dma((2,)),
             dma((chunks, max(space - 1, 1))),
             dma((chunks, space)),
             dma((chunks,)),
@@ -288,7 +303,7 @@
             dma((peers,)),
         ],
         compiler_params=pltpu.CompilerParams(
-            collective_id=0, has_side_effects=True, vmem_limit_bytes=40 * 2**20
+            collective_id=0, has_side_effects=True, vmem_limit_bytes=52 * 2**20
         ),
         name="spectra",
     )(snapshots, weight, table)

time: 66.5 us -> 64.5 us (0.970)
  local copies, waits for them, and re-layouts: 3.77 us -> 1.59 us
    unnamed x6 -> x4, local copies, waits for them, and re-layouts: 3.77 us -> 1.59 us
where the time goes in v1:
time: 64.5 us; the launch traced here: 64.3 us
  Pallas kernels  62.1 us (96%)
  local copies, waits for them, and re-layouts  1.59 us (2%)
  between operations  0.65 us (1%)
    pallas_call x1, Pallas kernels, on_device(): pl.pallas_call(functools.partial(spectra_kernel, exchange, space, tm, wei...  58.8 us
    pallas_call x1, Pallas kernels, on_device(): pl.pallas_call(functools.partial(modes_kernel, half), out_shape=(jax.Shap...  3.26 us
    unnamed x4, local copies, waits for them, and re-layouts  1.59 us

profile of v1, /device:TPU:0, one launch (start us, length us, event | category | flops | bytes accessed | tf_op | source)
XLA Modules:
  0.0 64.3 jit_solution(17241956619564347180)
XLA Ops:
  0.6 0.0 copy-start
  0.6 0.9 %copy-done = f32[2,64,256]{2,1,0:T(8,128)S(1)} copy-done((f32[2,64,256]{2,1,0:T(8,128)S(1)}, f32[2,64,256]{2,1,0:T(8,128)}, u32[]{:S(2)}) %copy-start) | copy-done | bytes 131096
  1.5 0.0 copy-start.1
  1.5 0.7 %copy-done.1 = f32[1024]{0:T(1024)S(1)} copy-done((f32[1024]{0:T(1024)S(1)}, f32[1024]{0:T(1024)}, u32[]{:S(2)}) %copy-start.1) | copy-done | bytes 4120
  2.2 58.8 %spectra.1 = (f32[256,1024]{1,0:T(8,128)S(1)}, f32[2,16,128]{2,1,0:T(8,128)S(1)}) custom-call(f32[16,16,4096]{2,1,0:T(8,128)} %snap.1, f32[2,1,512]{2,1,0:T(1,128)S(1)} %bitcast.1, f32[2,64,256]{2,1,0:T(8,128)S(1)} %copy-done), custom_call_target="tpu_custom_call" | custom-call | tf_op jit(solution)/shard_map/spectra/pallas_call | solution.py:278
  61.1 3.3 %modes.1 = (f32[8,2,16,1024]{3,2,1,0:T(8,128)}, f32[2,8,16,16]{3,2,1,0:T(8,128)}) custom-call(f32[2,16,128]{2,1,0:T(8,128)S(1)} %get-tuple-element.4.gram, f32[256,1024]{1,0:T(8,128)S(1)} %get-tuple-element.5.x), custom_call_target="tpu_custom_call" | custom-call | tf_op jit(solution)/shard_map/modes/pallas_call | solution.py:310
Async XLA Ops:
  0.6 0.9 %copy-start = (f32[2,64,256]{2,1,0:T(8,128)S(1)}, f32[2,64,256]{2,1,0:T(8,128)}, u32[]{:S(2)}) copy-start(f32[2,64,256]{2,1,0:T(8,128)} %constant.2.clone.table_in) | copy-start | bytes 393220
  1.5 0.7 %copy-start.1 = (f32[1024]{0:T(1024)S(1)}, f32[1024]{0:T(1024)}, u32[]{:S(2)}) copy-start(f32[1024]{0:T(1024)} %param.4) | copy-start | bytes 12292

commit v2 on v1

--- a/solution.py
+++ b/solution.py
@@ -199,7 +199,7 @@
     g_out[...] = acc * (1.0 / total)
 
 
-def modes_kernel(half, gram, x, modes, upper):
+def factor(half, gram, upper, big):
     nb, lanes = gram.shape[1], gram.shape[2]
     row = lax.broadcasted_iota(jnp.int32, (nb, lanes), 0)
     lane = lax.broadcasted_iota(jnp.int32, (nb, lanes), 1)
@@ -247,8 +247,15 @@
         fi = jnp.where(which == f, li, 0.0)
         parts.append(jnp.concatenate([fr, fi], axis=1))
         parts.append(jnp.concatenate([-fi, fr], axis=1))
-    big = jnp.concatenate(parts, axis=0)
-    out = jnp.dot(big, x[...], precision=HIGHEST, preferred_element_type=jnp.float32)
+    big[...] = jnp.concatenate(parts, axis=0)
+
+
+def modes_kernel(half, gram, x, modes, upper, big):
+    @pl.when(pl.program_id(0) == 0)
+    def _():
+        factor(half, gram, upper, big)
+
+    out = jnp.dot(big[...], x[...], precision=HIGHEST, preferred_element_type=jnp.float32)
     modes[...] = out.reshape(modes.shape)
 
 
@@ -313,8 +320,16 @@
             jax.ShapeDtypeStruct((half, 2, nb, freq * rows), jnp.float32),
             jax.ShapeDtypeStruct((2, half, nb, nb), jnp.float32),
         ),
-        in_specs=[vmem, vmem],
-        out_specs=(vmem, vmem),
+        grid=(2,),
+        in_specs=[
+            pl.BlockSpec((2, nb, lanes), lambda j: (0, 0, 0)),
+            pl.BlockSpec((2 * lanes, rows), lambda j: (0, j)),
+        ],
+        out_specs=(
+            pl.BlockSpec((half, 2, nb, rows), lambda j: (0, 0, 0, j)),
+            pl.BlockSpec((2, half, nb, nb), lambda j: (0, 0, 0, 0)),
+        ),
+        scratch_shapes=[pltpu.VMEM((2 * lanes, 2 * lanes), jnp.float32)],
         compiler_params=pltpu.CompilerParams(vmem_limit_bytes=40 * 2**20),
         name="modes",
     )(gram, x)

time: 64.5 us -> 64.8 us (level)
  no operation moved by 1% of the time
where the time goes in v2:
time: 64.8 us; the launch traced here: 64.6 us
  Pallas kernels  62.4 us (96%)
  local copies, waits for them, and re-layouts  1.59 us (2%)
  between operations  0.65 us (1%)
    pallas_call x1, Pallas kernels, on_device(): pl.pallas_call(functools.partial(spectra_kernel, exchange, space, tm, wei...  58.8 us
    pallas_call x1, Pallas kernels, on_device(): pl.pallas_call(functools.partial(modes_kernel, half), out_shape=(jax.Shap...  3.55 us
    unnamed x4, local copies, waits for them, and re-layouts  1.59 us

profile of v2, /device:TPU:0, one launch (start us, length us, event | category | flops | bytes accessed | tf_op | source)
XLA Modules:
  0.0 64.6 jit_solution(10067671888548005606)
XLA Ops:
  0.6 0.0 copy-start
  0.6 0.9 %copy-done = f32[2,64,256]{2,1,0:T(8,128)S(1)} copy-done((f32[2,64,256]{2,1,0:T(8,128)S(1)}, f32[2,64,256]{2,1,0:T(8,128)}, u32[]{:S(2)}) %copy-start) | copy-done | bytes 131096
  1.5 0.0 copy-start.1
  1.5 0.7 %copy-done.1 = f32[1024]{0:T(1024)S(1)} copy-done((f32[1024]{0:T(1024)S(1)}, f32[1024]{0:T(1024)}, u32[]{:S(2)}) %copy-start.1) | copy-done | bytes 4120
  2.2 58.8 %spectra.1 = (f32[256,1024]{1,0:T(8,128)S(1)}, f32[2,16,128]{2,1,0:T(8,128)S(1)}) custom-call(f32[16,16,4096]{2,1,0:T(8,128)} %snap.1, f32[2,1,512]{2,1,0:T(1,128)S(1)} %bitcast.1, f32[2,64,256]{2,1,0:T(8,128)S(1)} %copy-done), custom_call_target="tpu_custom_call" | custom-call | tf_op jit(solution)/shard_map/spectra/pallas_call | solution.py:285
  61.1 3.5 %modes.1 = (f32[8,2,16,1024]{3,2,1,0:T(8,128)}, f32[2,8,16,16]{3,2,1,0:T(8,128)}) custom-call(f32[2,16,128]{2,1,0:T(8,128)S(1)} %get-tuple-element.4.gram, f32[256,1024]{1,0:T(8,128)S(1)} %get-tuple-element.5.x), custom_call_target="tpu_custom_call" | custom-call | tf_op jit(solution)/shard_map/modes/pallas_call | solution.py:317
Async XLA Ops:
  0.6 0.9 %copy-start = (f32[2,64,256]{2,1,0:T(8,128)S(1)}, f32[2,64,256]{2,1,0:T(8,128)}, u32[]{:S(2)}) copy-start(f32[2,64,256]{2,1,0:T(8,128)} %constant.2.clone.table_in) | copy-start | bytes 393220
  1.5 0.7 %copy-start.1 = (f32[1024]{0:T(1024)S(1)}, f32[1024]{0:T(1024)}, u32[]{:S(2)}) copy-start(f32[1024]{0:T(1024)} %param.4) | copy-start | bytes 12292
